TPU v7x, 256 devices: a whole 4x4x8 slice. The times are simulated.
256 devices in a mesh: seg: 8 (over x_hi, y), elem: 32 (over x_lo, z, core).
Axes of the slice: x: 4 (x_hi: 2, x_lo: 2; x = x_hi * 2 + x_lo), y: 4, z: 8, core: 2. Of those that a mesh axis runs over, the one named last changes fastest.
Arguments:
- base_flow: float32 [8, 3, 64, 8192], P('seg', None, None, 'elem'), may hold values from -3 to 3
- probe_field: float32 [8, 3, 64, 8192], P('seg', None, None, 'elem'), may hold values from -6 to 6
- neighbours: int32 [6, 8192], P(None, 'elem'), may hold values from 0 to 8191, as said below
- face_codes: int32 [6, 8192], P(None, 'elem'), may hold values from 0 to 23, as said below
- face_counts: int32 [8192], P('elem'), may hold values from 2 to 6
Outputs:
- first_image: float32 [8, 3, 64, 8192], P('seg', None, None, 'elem')
- second_image: float32 [8, 3, 64, 8192], P('seg', None, None, 'elem')
Inputs may be any that keep to these rules, and one draw needn't show every extreme that they name: `neighbours`: every element's neighbour in every slot, used or not, lies within 64 places of the element's own index, counted cyclically over 8192. `face_codes`: each code is 4 times a face number plus a rotation; slots past an element's count hold leftover entries.
All inputs are finite; a program needn't handle non-finite values.
Results may differ from a plain program's by a relative error of at most 0.0001.
Values sent between devices are 32-bit elements; how exact they have to be, the bound alone decides.
A program may use at most 128 MiB of HBM per device.

v0:
```python
import functools

import jax
import jax.numpy as jnp
import ml_dtypes
import numpy as np
from jax import lax
from jax.experimental import pallas as pl
from jax.experimental.pallas import tpu as pltpu
from jax.sharding import PartitionSpec as P

STEPS = 2
VISCOSITY = 0.05
PENALTY = 1.0
TIME_STEP = 0.05

COMP = 3
NODES = 64
SHARD = 256
LANES = 128
HALO = 64
CODES = 24


def operator_tables():
    points = np.array([-1.0, -1.0 / np.sqrt(5.0), 1.0 / np.sqrt(5.0), 1.0])
    barycentric = np.array(
        [
            1.0 / np.prod([points[row] - points[col] for col in range(4) if col != row])
            for row in range(4)
        ]
    )
    derivative = np.zeros((4, 4))
    for row in range(4):
        for col in range(4):
            if row != col:
                derivative[row, col] = (
                    barycentric[col] / barycentric[row] / (points[row] - points[col])
                )
        derivative[row, row] = -np.sum(derivative[row])
    identity = np.eye(4)
    gradient = [
        np.kron(np.kron(derivative, identity), identity),
        np.kron(np.kron(identity, derivative), identity),
        np.kron(np.kron(identity, identity), derivative),
    ]
    laplacian = sum(table @ table for table in gradient)
    return gradient, laplacian


def face_nodes(which_face):
    grid = np.arange(NODES).reshape(4, 4, 4)
    return np.take(grid, 0 if which_face % 2 == 0 else 3, axis=which_face // 2)


def constant_tables():
    gradient, laplacian = operator_tables()
    stacked = np.concatenate([VISCOSITY * laplacian] + gradient, axis=0)
    high = stacked.astype(ml_dtypes.bfloat16)
    low = (stacked - high.astype(np.float64)).astype(ml_dtypes.bfloat16)
    operators = np.concatenate([high, high, low, low], axis=1)
    select = np.zeros((CODES * 16, NODES))
    lift = np.zeros((NODES, 96))
    for face in range(6):
        for turn in range(4):
            nodes = np.rot90(face_nodes(face ^ 1), turn).ravel()
            for place, node in enumerate(nodes):
                select[(4 * face + turn) * 16 + place, node] = 1.0
        for place, node in enumerate(face_nodes(face).ravel()):
            lift[node, face * 16 + place] = 1.0
    lift = np.concatenate([lift, lift], axis=1)
    return (
        jnp.asarray(operators),
        jnp.asarray(select.astype(ml_dtypes.bfloat16)),
        jnp.asarray(lift.astype(ml_dtypes.bfloat16)),
    )


def split(value):
    high = value.astype(jnp.bfloat16)
    low = (value - high.astype(jnp.float32)).astype(jnp.bfloat16)
    return high, low


def dot(left, right):
    return jnp.dot(left, right, preferred_element_type=jnp.float32)


def kernel(
    segs,
    elems,
    base_ref,
    probe_ref,
    near_ref,
    code_ref,
    count_ref,
    oper_ref,
    sel_ref,
    lift_ref,
    first_ref,
    second_ref,
    state,
    acc,
    base_grad,
    own_count,
    gather,
    traces,
    jumps,
    mixed,
    send_buf,
    halo_buf,
    follow,
    halo_send,
    halo_recv,
    follow_send,
    follow_recv,
):
    seg = lax.axis_index("seg")
    elem = lax.axis_index("elem")
    right = lax.rem(elem + 1, elems)
    left = lax.rem(elem + elems - 1, elems)
    ahead = lax.rem(seg + 1, segs)
    behind = lax.rem(seg + segs - 1, segs)
    barrier = pltpu.get_barrier_semaphore()
    for target in ({"elem": left}, {"elem": right}, {"seg": ahead}):
        pl.semaphore_signal(
            barrier, inc=1, device_id=target, device_id_type=pl.DeviceIdType.MESH
        )

    lane_low = lax.broadcasted_iota(jnp.int32, (96, LANES), 1) < HALO

    def halo_copy(step, side):
        return pltpu.make_async_remote_copy(
            src_ref=send_buf.at[step, side],
            dst_ref=halo_buf.at[step, side],
            send_sem=halo_send.at[step, side],
            recv_sem=halo_recv.at[step, side],
            device_id={"elem": (right, left)[side]},
            device_id_type=pl.DeviceIdType.MESH,
        )

    def pack_halo(step):
        upper = state[96:192, LANES:SHARD]
        send_buf[step, 0] = jnp.where(
            lane_low, pltpu.roll(upper, HALO, 1), state[0:96, LANES:SHARD]
        )
        lower = state[96:192, 0:LANES]
        send_buf[step, 1] = jnp.where(
            lane_low, state[0:96, 0:LANES], pltpu.roll(lower, HALO, 1)
        )

    def follow_copy(image, source):
        return pltpu.make_async_remote_copy(
            src_ref=source,
            dst_ref=follow.at[image],
            send_sem=follow_send.at[image],
            recv_sem=follow_recv.at[image],
            device_id={"seg": behind},
            device_id_type=pl.DeviceIdType.MESH,
        )

    state[...] = probe_ref[...].reshape(COMP * NODES, SHARD)
    pack_halo(0)
    pl.semaphore_wait(barrier, 3)
    for side in range(2):
        halo_copy(0, side).start()
    follow_copy(0, probe_ref).start()

    first_block = elem * (SHARD // LANES)
    rows16 = lax.broadcasted_iota(jnp.int32, (LANES, LANES), 0)
    for block in range(2):
        lanes = slice(block * LANES, (block + 1) * LANES)
        near = near_ref[:, lanes]
        count = count_ref[:, lanes]
        slot = lax.broadcasted_iota(jnp.int32, (6, LANES), 0)
        code = jnp.where(slot < count, code_ref[:, lanes], -1)
        place = jnp.bitwise_and(near, LANES - 1)
        is_own = jnp.right_shift(near, 7) == first_block + block
        for part in range(2):
            chosen = jnp.where(is_own, place, -1) if part == 0 else jnp.where(is_own, -1, place)
            hot = [
                jnp.where(rows16 == chosen[k : k + 1], 1.0, 0.0).astype(jnp.bfloat16)
                for k in range(6)
            ]

            def build(which, carry):
                total = None
                for k in range(6):
                    match = jnp.where(code[k : k + 1] == which, 1.0, 0.0)
                    match = jnp.broadcast_to(match, (16, LANES)).astype(jnp.bfloat16)
                    match = jnp.concatenate([match] * 8, axis=0)
                    term = hot[k] * match
                    total = term if total is None else total + term
                gather[part, block, which] = total
                return carry

            lax.fori_loop(0, CODES, build, 0)
        node = lax.broadcasted_iota(jnp.int32, (NODES, LANES), 0)
        digits = (
            jnp.right_shift(node, 4),
            jnp.bitwise_and(jnp.right_shift(node, 2), 3),
            jnp.bitwise_and(node, 3),
        )
        total = jnp.zeros((NODES, LANES), jnp.float32)
        for face in range(6):
            hits = jnp.zeros((1, LANES), jnp.float32)
            for k in range(6):
                match = jnp.logical_and(
                    code[k : k + 1] >= 4 * face, code[k : k + 1] < 4 * face + 4
                )
                hits = hits + jnp.where(match, 1.0, 0.0)
            on_face = digits[face // 2] == (0 if face % 2 == 0 else 3)
            total = total + jnp.where(on_face, hits, 0.0)
        own_count[:, lanes] = total

    def derivatives(high, low):
        return dot(oper_ref[...], jnp.concatenate([high, low, high, low], axis=0))

    for comp in range(COMP):
        high, low = split(base_ref[comp])
        grads = derivatives(high, low)
        for d in range(3):
            base_grad[d, comp] = grads[(d + 1) * NODES : (d + 2) * NODES]

    def fill_traces(comp, high, low):
        for piece, value in enumerate((high, low)):
            picked = dot(sel_ref[...], value).astype(jnp.bfloat16)
            traces[:, 2 * comp + piece] = picked.reshape(CODES, 16, SHARD)

    def gather_jumps(part):
        for face in range(6):
            for block in range(2):
                lanes = slice(block * LANES, (block + 1) * LANES)
                sources = jnp.concatenate(
                    [
                        traces[4 * face + turn, :, :, lanes].reshape(96, LANES)
                        for turn in range(4)
                    ],
                    axis=1,
                )
                table = gather[part, block, 4 * face : 4 * face + 4].reshape(4 * LANES, LANES)
                found = dot(sources, table)
                for comp in range(COMP):
                    value = (
                        found[32 * comp : 32 * comp + 16] + found[32 * comp + 16 : 32 * comp + 32]
                    )
                    rows = slice(16 * face, 16 * face + 16)
                    if part == 0:
                        jumps[comp, rows, lanes] = value
                    else:
                        jumps[comp, rows, lanes] += value

    def advance(step, carry):
        for comp in range(COMP):
            field = state[comp * NODES : (comp + 1) * NODES]
            high, low = split(field)
            grads = derivatives(high, low)
            total = grads[0:NODES] - own_count[...] * field
            for d in range(3):
                total = total - base_ref[d] * grads[(d + 1) * NODES : (d + 2) * NODES]
            for d in range(3):
                total = total - state[d * NODES : (d + 1) * NODES] * base_grad[d, comp]
            acc[comp] = total
            fill_traces(comp, high, low)
        gather_jumps(0)

        for side in range(2):
            halo_copy(step, side).wait()
        from_left = halo_buf[step, 0]
        from_right = halo_buf[step, 1]
        mixed[0:96, 0:LANES] = jnp.where(lane_low, state[0:96, LANES:SHARD], from_left)
        mixed[96:192, 0:LANES] = jnp.where(
            lane_low, state[96:192, LANES:SHARD], pltpu.roll(from_left, HALO, 1)
        )
        mixed[0:96, LANES:SHARD] = jnp.where(lane_low, from_right, state[0:96, 0:LANES])
        mixed[96:192, LANES:SHARD] = jnp.where(
            lane_low, pltpu.roll(from_right, HALO, 1), state[96:192, 0:LANES]
        )
        for comp in range(COMP):
            high, low = split(mixed[comp * NODES : (comp + 1) * NODES])
            fill_traces(comp, high, low)
        gather_jumps(1)

        for comp in range(COMP):
            high, low = split(jumps[comp])
            flux = dot(lift_ref[...], jnp.concatenate([high, low], axis=0))
            rows = slice(comp * NODES, (comp + 1) * NODES)
            state[rows] = state[rows] + TIME_STEP * (acc[comp] + PENALTY * flux)

        for image, result in enumerate((first_ref, second_ref)):

            @pl.when(step == STEPS * (image + 1) - 1)
            def _():
                source = probe_ref if image == 0 else first_ref
                follow_copy(image, source).wait()
                value = state[...] - follow[image].reshape(COMP * NODES, SHARD)
                result[...] = value.reshape(COMP, NODES, SHARD)
                if image == 0:
                    state[...] = value
                    follow_copy(1, first_ref).start()

        @pl.when(step < 2 * STEPS - 1)
        def _():
            pack_halo(step + 1)
            for side in range(2):
                halo_copy(step + 1, side).start()

        return carry

    lax.fori_loop(0, 2 * STEPS, advance, 0)


def on_device(base_flow, probe_field, neighbours, face_codes, face_counts):
    operators, select, lift = constant_tables()
    field = jax.ShapeDtypeStruct((COMP, NODES, SHARD), jnp.float32)
    vmem = pl.BlockSpec(memory_space=pltpu.VMEM)
    first_image, second_image = pl.pallas_call(
        functools.partial(kernel, lax.axis_size("seg"), lax.axis_size("elem")),
        out_shape=(field, field),
        in_specs=[vmem] * 8,
        out_specs=(vmem, vmem),
        scratch_shapes=[
            pltpu.VMEM((COMP * NODES, SHARD), jnp.float32),
            pltpu.VMEM((COMP, NODES, SHARD), jnp.float32),
            pltpu.VMEM((3, COMP, NODES, SHARD), jnp.float32),
            pltpu.VMEM((NODES, SHARD), jnp.float32),
            pltpu.VMEM((2, 2, CODES, LANES, LANES), jnp.bfloat16),
            pltpu.VMEM((CODES, 2 * COMP, 16, SHARD), jnp.bfloat16),
            pltpu.VMEM((COMP, 96, SHARD), jnp.float32),
            pltpu.VMEM((COMP * NODES, SHARD), jnp.float32),
            pltpu.VMEM((2 * STEPS, 2, 96, LANES), jnp.float32),
            pltpu.VMEM((2 * STEPS, 2, 96, LANES), jnp.float32),
            pltpu.VMEM((2, COMP, NODES, SHARD), jnp.float32),
            pltpu.SemaphoreType.DMA((2 * STEPS, 2)),
            pltpu.SemaphoreType.DMA((2 * STEPS, 2)),
            pltpu.SemaphoreType.DMA((2,)),
            pltpu.SemaphoreType.DMA((2,)),
        ],
        compiler_params=pltpu.CompilerParams(
            collective_id=0, has_side_effects=True, vmem_limit_bytes=40 * 1024 * 1024
        ),
        name="shooting",
    )(
        base_flow[0],
        probe_field[0],
        neighbours,
        face_codes,
        face_counts.reshape(1, SHARD),
        operators,
        select,
        lift,
    )
    return (first_image[None], second_image[None])


def solution(mesh):
    placed = (
        P("seg", None, None, "elem"),
        P("seg", None, None, "elem"),
        P(None, "elem"),
        P(None, "elem"),
        P("elem"),
    )
    return jax.shard_map(
        on_device,
        mesh=mesh,
        in_specs=placed,
        out_specs=(P("seg", None, None, "elem"), P("seg", None, None, "elem")),
        check_vma=False,
    )
```

profile of v0, /device:TPU:2, one launch (start us, length us, event | category | flops | bytes accessed | tf_op | source)
XLA Modules:
  0.0 36.7 jit_solution(10251652717755258251)
XLA Ops:
  0.6 0.0 copy-start.7
  0.6 0.7 %copy-done.7 = s32[256]{0:T(256)S(1)} copy-done((s32[256]{0:T(256)S(1)}, s32[256]{0:T(256)}, u32[]{:S(2)}) %copy-start.7) | copy-done | bytes 1048
  1.3 0.0 copy-start
  1.3 0.9 %copy-done = f32[1,3,64,256]{3,2,1,0:T(8,128)S(1)} copy-done((f32[1,3,64,256]{3,2,1,0:T(8,128)S(1)}, f32[1,3,64,256]{3,2,1,0:T(8,128)}, u32[]{:S(2)}) %copy-start) | copy-done | bytes 196632
  2.2 0.0 copy-start.1
  2.2 0.9 %copy-done.1 = f32[1,3,64,256]{3,2,1,0:T(8,128)S(1)} copy-done((f32[1,3,64,256]{3,2,1,0:T(8,128)S(1)}, f32[1,3,64,256]{3,2,1,0:T(8,128)}, u32[]{:S(2)}) %copy-start.1) | copy-done | bytes 196632
  3.2 0.0 copy-start.2
  3.2 0.9 %copy-done.2 = bf16[256,256]{1,0:T(8,128)(2,1)S(1)} copy-done((bf16[256,256]{1,0:T(8,128)(2,1)S(1)}, bf16[256,256]{1,0:T(8,128)(2,1)}, u32[]{:S(2)}) %copy-start.2) | copy-done | bytes 131096
  4.1 0.0 copy-start.3
  4.1 0.9 %copy-done.3 = bf16[384,64]{1,0:T(8,128)(2,1)S(1)} copy-done((bf16[384,64]{1,0:T(8,128)(2,1)S(1)}, bf16[384,64]{1,0:T(8,128)(2,1)}, u32[]{:S(2)}) %copy-start.3) | copy-done | bytes 49176
  5.0 0.0 copy-start.4
  5.0 0.8 %copy-done.4 = bf16[64,192]{1,0:T(8,128)(2,1)S(1)} copy-done((bf16[64,192]{1,0:T(8,128)(2,1)S(1)}, bf16[64,192]{1,0:T(8,128)(2,1)}, u32[]{:S(2)}) %copy-start.4) | copy-done | bytes 24600
  5.7 0.0 copy-start.5
  5.7 0.7 %copy-done.5 = s32[6,256]{1,0:T(8,128)S(1)} copy-done((s32[6,256]{1,0:T(8,128)S(1)}, s32[6,256]{1,0:T(8,128)}, u32[]{:S(2)}) %copy-start.5) | copy-done | bytes 6168
  6.4 0.0 copy-start.6
  6.4 0.7 %copy-done.6 = s32[6,256]{1,0:T(8,128)S(1)} copy-done((s32[6,256]{1,0:T(8,128)S(1)}, s32[6,256]{1,0:T(8,128)}, u32[]{:S(2)}) %copy-start.6) | copy-done | bytes 6168
  7.1 28.2 %shooting.1 = (f32[3,64,256]{2,1,0:T(8,128)S(1)}, f32[3,64,256]{2,1,0:T(8,128)S(1)}) custom-call(f32[3,64,256]{2,1,0:T(8,128)S(1)} %bitcast.7, f32[3,64,256]{2,1,0:T(8,128)S(1)} %bitcast.8, s32[6,256]{1,0:T(8,128)S(1)} %copy-done.5, s32[6,256]{1,0:T(8,128)S(1)} %copy-done.6, s32[1,256]{1,0:T(1,128)S(1)} %bitcast.9, bf16[256,256]{1,0:T(8,128)(2,1)S(1)} %copy-done.2, ...), custom_call_target="tpu_custom_call" | custom-call | tf_op jit(solution)/shard_map/shooting/pallas_call | solution.py:317
  35.4 0.7 %copy.12 = f32[1,3,64,256]{3,2,1,0:T(8,128)} copy(f32[1,3,64,256]{3,2,1,0:T(8,128)S(1)} %bitcast.6) | data formatting | bytes 393216
  36.0 0.7 %copy.13 = f32[1,3,64,256]{3,2,1,0:T(8,128)} copy(f32[1,3,64,256]{3,2,1,0:T(8,128)S(1)} %bitcast.5) | data formatting | bytes 393216
Async XLA Ops:
  0.6 0.7 %copy-start.7 = (s32[256]{0:T(256)S(1)}, s32[256]{0:T(256)}, u32[]{:S(2)}) copy-start(s32[256]{0:T(256)} %param.12) | copy-start | bytes 3076
  1.3 0.9 %copy-start = (f32[1,3,64,256]{3,2,1,0:T(8,128)S(1)}, f32[1,3,64,256]{3,2,1,0:T(8,128)}, u32[]{:S(2)}) copy-start(f32[1,3,64,256]{3,2,1,0:T(8,128)} %param.8) | copy-start | bytes 589828
  2.2 0.9 %copy-start.1 = (f32[1,3,64,256]{3,2,1,0:T(8,128)S(1)}, f32[1,3,64,256]{3,2,1,0:T(8,128)}, u32[]{:S(2)}) copy-start(f32[1,3,64,256]{3,2,1,0:T(8,128)} %param.9) | copy-start | bytes 589828
  3.2 0.9 %copy-start.2 = (bf16[256,256]{1,0:T(8,128)(2,1)S(1)}, bf16[256,256]{1,0:T(8,128)(2,1)}, u32[]{:S(2)}) copy-start(bf16[256,256]{1,0:T(8,128)(2,1)} %constant.6.clone.oper_ref) | copy-start | bytes 393220
  4.1 0.9 %copy-start.3 = (bf16[384,64]{1,0:T(8,128)(2,1)S(1)}, bf16[384,64]{1,0:T(8,128)(2,1)}, u32[]{:S(2)}) copy-start(bf16[384,64]{1,0:T(8,128)(2,1)} %constant.7.clone.sel_ref) | copy-start | bytes 147460
  5.0 0.8 %copy-start.4 = (bf16[64,192]{1,0:T(8,128)(2,1)S(1)}, bf16[64,192]{1,0:T(8,128)(2,1)}, u32[]{:S(2)}) copy-start(bf16[64,192]{1,0:T(8,128)(2,1)} %constant.8.clone.lift_ref) | copy-start | bytes 73732
  5.7 0.7 %copy-start.5 = (s32[6,256]{1,0:T(8,128)S(1)}, s32[6,256]{1,0:T(8,128)}, u32[]{:S(2)}) copy-start(s32[6,256]{1,0:T(8,128)} %near_ref.1) | copy-start | bytes 18436
  6.4 0.7 %copy-start.6 = (s32[6,256]{1,0:T(8,128)S(1)}, s32[6,256]{1,0:T(8,128)}, u32[]{:S(2)}) copy-start(s32[6,256]{1,0:T(8,128)} %code_ref.1) | copy-start | bytes 18436
where the time goes:
time: 37.1 us; the launch traced here: 36.7 us
  Pallas kernels  28.2 us (76%)
  local copies, waits for them, and re-layouts  7.83 us (21%)
  between operations  0.66 us (2%)
    pallas_call x1, Pallas kernels, on_device(): pl.pallas_call(functools.partial(kernel, lax.axis_size('seg'), lax.axis_s...  28.2 us
    unnamed x18, local copies, waits for them, and re-layouts  7.83 us

commit v1 on v0

--- a/solution.py
+++ b/solution.py
@@ -20,6 +20,7 @@
 LANES = 128
 HALO = 64
 CODES = 24
+TRACES = 24
 
 
 def operator_tables():
@@ -53,21 +54,41 @@
     return np.take(grid, 0 if which_face % 2 == 0 else 3, axis=which_face // 2)
 
 
+def orbit_places():
+    turned = np.rot90(np.arange(16).reshape(4, 4), 1).ravel()
+    seen, starts = set(), []
+    for place in range(16):
+        if place not in seen:
+            starts.append(place)
+            for _ in range(4):
+                seen.add(place)
+                place = turned[place]
+    rows = [starts]
+    for _ in range(3):
+        rows.append([turned[place] for place in rows[-1]])
+    return np.array(rows).ravel()
+
+
 def constant_tables():
     gradient, laplacian = operator_tables()
     stacked = np.concatenate([VISCOSITY * laplacian] + gradient, axis=0)
     high = stacked.astype(ml_dtypes.bfloat16)
     low = (stacked - high.astype(np.float64)).astype(ml_dtypes.bfloat16)
     operators = np.concatenate([high, high, low, low], axis=1)
-    select = np.zeros((CODES * 16, NODES))
+    places = orbit_places()
+    select = np.zeros((2, 6, 2, 2, 8, 2, NODES))
     lift = np.zeros((NODES, 96))
     for face in range(6):
-        for turn in range(4):
-            nodes = np.rot90(face_nodes(face ^ 1), turn).ravel()
-            for place, node in enumerate(nodes):
-                select[(4 * face + turn) * 16 + place, node] = 1.0
-        for place, node in enumerate(face_nodes(face).ravel()):
-            lift[node, face * 16 + place] = 1.0
+        source = face_nodes(face ^ 1).ravel()[places]
+        target = face_nodes(face).ravel()[places]
+        for turn in range(2):
+            for place in range(16):
+                node = source[(place + 4 * turn) % 16]
+                for piece in range(2):
+                    select[turn, face, place // 8, piece, place % 8, piece, node] = 1.0
+        for place in range(16):
+            lift[target[place], face * 16 + place] = 1.0
+    select = select.reshape(TRACES * 16, 2 * NODES)
     lift = np.concatenate([lift, lift], axis=1)
     return (
         jnp.asarray(operators),
@@ -89,6 +110,16 @@
 def kernel(
     segs,
     elems,
+    base_in,
+    probe_in,
+    near_in,
+    code_in,
+    count_in,
+    oper_in,
+    sel_in,
+    lift_in,
+    first_ref,
+    second_ref,
     base_ref,
     probe_ref,
     near_ref,
@@ -97,19 +128,19 @@
     oper_ref,
     sel_ref,
     lift_ref,
-    first_ref,
-    second_ref,
     state,
     acc,
     base_grad,
     own_count,
-    gather,
-    traces,
+    gather_own,
+    gather_halo,
+    trace_own,
+    trace_halo,
     jumps,
-    mixed,
     send_buf,
     halo_buf,
     follow,
+    input_sem,
     halo_send,
     halo_recv,
     follow_send,
@@ -126,6 +157,23 @@
         pl.semaphore_signal(
             barrier, inc=1, device_id=target, device_id_type=pl.DeviceIdType.MESH
         )
+    loads = [
+        pltpu.make_async_copy(source, target, input_sem.at[index])
+        for index, (source, target) in enumerate(
+            (
+                (probe_in, probe_ref),
+                (near_in, near_ref),
+                (code_in, code_ref),
+                (count_in, count_ref),
+                (base_in, base_ref),
+                (oper_in, oper_ref),
+                (sel_in, sel_ref),
+                (lift_in, lift_ref),
+            )
+        )
+    ]
+    for load in loads:
+        load.start()
 
     lane_low = lax.broadcasted_iota(jnp.int32, (96, LANES), 1) < HALO
 
@@ -159,6 +207,7 @@
             device_id_type=pl.DeviceIdType.MESH,
         )
 
+    loads[0].wait()
     state[...] = probe_ref[...].reshape(COMP * NODES, SHARD)
     pack_halo(0)
     pl.semaphore_wait(barrier, 3)
@@ -166,41 +215,69 @@
         halo_copy(0, side).start()
     follow_copy(0, probe_ref).start()
 
+    for load in loads[1:4]:
+        load.wait()
     first_block = elem * (SHARD // LANES)
-    rows16 = lax.broadcasted_iota(jnp.int32, (LANES, LANES), 0)
+    row = lax.broadcasted_iota(jnp.int32, (LANES, LANES), 0)
+    codes, hots = [], []
     for block in range(2):
         lanes = slice(block * LANES, (block + 1) * LANES)
         near = near_ref[:, lanes]
-        count = count_ref[:, lanes]
         slot = lax.broadcasted_iota(jnp.int32, (6, LANES), 0)
-        code = jnp.where(slot < count, code_ref[:, lanes], -1)
+        codes.append(jnp.where(slot < count_ref[:, lanes], code_ref[:, lanes], -1))
         place = jnp.bitwise_and(near, LANES - 1)
         is_own = jnp.right_shift(near, 7) == first_block + block
-        for part in range(2):
-            chosen = jnp.where(is_own, place, -1) if part == 0 else jnp.where(is_own, -1, place)
-            hot = [
-                jnp.where(rows16 == chosen[k : k + 1], 1.0, 0.0).astype(jnp.bfloat16)
-                for k in range(6)
-            ]
-
-            def build(which, carry):
-                total = None
+        for chosen in (jnp.where(is_own, place, -1), jnp.where(is_own, -1, place)):
+            hots.append(
+                [
+                    jnp.where(row == chosen[k : k + 1], 1.0, 0.0).astype(jnp.bfloat16)
+                    for k in range(6)
+                ]
+            )
+
+    def build(face, carry):
+        empty = jnp.zeros((HALO, LANES), jnp.bfloat16)
+        for turn in range(4):
+            which = 4 * face + turn
+            for block in range(2):
+                lanes = slice(block * LANES, (block + 1) * LANES)
+                matches = []
                 for k in range(6):
-                    match = jnp.where(code[k : k + 1] == which, 1.0, 0.0)
+                    match = jnp.where(codes[block][k : k + 1] == which, 1.0, 0.0)
                     match = jnp.broadcast_to(match, (16, LANES)).astype(jnp.bfloat16)
-                    match = jnp.concatenate([match] * 8, axis=0)
-                    term = hot[k] * match
-                    total = term if total is None else total + term
-                gather[part, block, which] = total
-                return carry
-
-            lax.fori_loop(0, CODES, build, 0)
-        node = lax.broadcasted_iota(jnp.int32, (NODES, LANES), 0)
-        digits = (
-            jnp.right_shift(node, 4),
-            jnp.bitwise_and(jnp.right_shift(node, 2), 3),
-            jnp.bitwise_and(node, 3),
-        )
+                    matches.append(jnp.concatenate([match] * 8, axis=0))
+                totals = []
+                for part in range(2):
+                    total = None
+                    for k in range(6):
+                        term = hots[2 * block + part][k] * matches[k]
+                        total = term if total is None else total + term
+                    totals.append(total)
+                own, mixed = totals
+                if block == 0:
+                    gather_own[which, 0:128, lanes] = own
+                    gather_own[which, 128:192, lanes] = mixed[0:64]
+                    gather_own[which, 192:256, lanes] = empty
+                    gather_halo[which, 0:64, lanes] = empty
+                    gather_halo[which, 64:128, lanes] = mixed[64:128]
+                else:
+                    gather_own[which, 0:64, lanes] = empty
+                    gather_own[which, 64:128, lanes] = mixed[64:128]
+                    gather_own[which, 128:256, lanes] = own
+                    gather_halo[which, 0:64, lanes] = mixed[0:64]
+                    gather_halo[which, 64:128, lanes] = empty
+        return carry
+
+    lax.fori_loop(0, 6, build, 0)
+
+    node = lax.broadcasted_iota(jnp.int32, (NODES, LANES), 0)
+    digits = (
+        jnp.right_shift(node, 4),
+        jnp.bitwise_and(jnp.right_shift(node, 2), 3),
+        jnp.bitwise_and(node, 3),
+    )
+    for block in range(2):
+        code = codes[block]
         total = jnp.zeros((NODES, LANES), jnp.float32)
         for face in range(6):
             hits = jnp.zeros((1, LANES), jnp.float32)
@@ -211,7 +288,10 @@
                 hits = hits + jnp.where(match, 1.0, 0.0)
             on_face = digits[face // 2] == (0 if face % 2 == 0 else 3)
             total = total + jnp.where(on_face, hits, 0.0)
-        own_count[:, lanes] = total
+        own_count[:, block * LANES : (block + 1) * LANES] = total
+
+    for load in loads[4:8]:
+        load.wait()
 
     def derivatives(high, low):
         return dot(oper_ref[...], jnp.concatenate([high, low, high, low], axis=0))
@@ -222,33 +302,35 @@
         for d in range(3):
             base_grad[d, comp] = grads[(d + 1) * NODES : (d + 2) * NODES]
 
-    def fill_traces(comp, high, low):
-        for piece, value in enumerate((high, low)):
-            picked = dot(sel_ref[...], value).astype(jnp.bfloat16)
-            traces[:, 2 * comp + piece] = picked.reshape(CODES, 16, SHARD)
-
-    def gather_jumps(part):
+    def fill_traces(traces, comp, high, low):
+        picked = dot(sel_ref[...], jnp.concatenate([high, low], axis=0))
+        picked = picked.astype(jnp.bfloat16).reshape(TRACES, 16, high.shape[1])
+        traces[:, 16 * comp : 16 * comp + 16] = picked
+
+    def gather_jumps(traces, tables, add):
         for face in range(6):
-            for block in range(2):
-                lanes = slice(block * LANES, (block + 1) * LANES)
-                sources = jnp.concatenate(
-                    [
-                        traces[4 * face + turn, :, :, lanes].reshape(96, LANES)
-                        for turn in range(4)
-                    ],
-                    axis=1,
-                )
-                table = gather[part, block, 4 * face : 4 * face + 4].reshape(4 * LANES, LANES)
-                found = dot(sources, table)
+            sources = []
+            for turn in range(4):
+                pair = 2 * (6 * (turn % 2) + face)
+                for half in range(2):
+                    sources.append(traces[pair + (half + turn // 2) % 2])
+            sources = jnp.concatenate(
+                [
+                    jnp.concatenate(sources[2 * turn : 2 * turn + 2], axis=0)
+                    for turn in range(4)
+                ],
+                axis=1,
+            )
+            table = tables[4 * face : 4 * face + 4]
+            found = dot(sources, table.reshape(4 * table.shape[1], SHARD))
+            for half in range(2):
                 for comp in range(COMP):
-                    value = (
-                        found[32 * comp : 32 * comp + 16] + found[32 * comp + 16 : 32 * comp + 32]
-                    )
-                    rows = slice(16 * face, 16 * face + 16)
-                    if part == 0:
-                        jumps[comp, rows, lanes] = value
-                    else:
-                        jumps[comp, rows, lanes] += value
+                    at = 48 * half + 16 * comp
+                    value = found[at : at + 8] + found[at + 8 : at + 16]
+                    rows = slice(16 * face + 8 * half, 16 * face + 8 * half + 8)
+                    if add:
+                        value = value + jumps[comp, rows]
+                    jumps[comp, rows] = value
 
     def advance(step, carry):
         for comp in range(COMP):
@@ -261,25 +343,24 @@
             for d in range(3):
                 total = total - state[d * NODES : (d + 1) * NODES] * base_grad[d, comp]
             acc[comp] = total
-            fill_traces(comp, high, low)
-        gather_jumps(0)
+            fill_traces(trace_own, comp, high, low)
+        gather_jumps(trace_own, gather_own, False)
 
         for side in range(2):
             halo_copy(step, side).wait()
         from_left = halo_buf[step, 0]
         from_right = halo_buf[step, 1]
-        mixed[0:96, 0:LANES] = jnp.where(lane_low, state[0:96, LANES:SHARD], from_left)
-        mixed[96:192, 0:LANES] = jnp.where(
-            lane_low, state[96:192, LANES:SHARD], pltpu.roll(from_left, HALO, 1)
-        )
-        mixed[0:96, LANES:SHARD] = jnp.where(lane_low, from_right, state[0:96, 0:LANES])
-        mixed[96:192, LANES:SHARD] = jnp.where(
-            lane_low, pltpu.roll(from_right, HALO, 1), state[96:192, 0:LANES]
+        halo = jnp.concatenate(
+            [
+                jnp.where(lane_low, from_right, from_left),
+                pltpu.roll(jnp.where(lane_low, from_left, from_right), HALO, 1),
+            ],
+            axis=0,
         )
         for comp in range(COMP):
-            high, low = split(mixed[comp * NODES : (comp + 1) * NODES])
-            fill_traces(comp, high, low)
-        gather_jumps(1)
+            high, low = split(halo[comp * NODES : (comp + 1) * NODES])
+            fill_traces(trace_halo, comp, high, low)
+        gather_jumps(trace_halo, gather_halo, True)
 
         for comp in range(COMP):
             high, low = split(jumps[comp])
@@ -297,13 +378,16 @@
                 result[...] = value.reshape(COMP, NODES, SHARD)
                 if image == 0:
                     state[...] = value
-                    follow_copy(1, first_ref).start()
 
         @pl.when(step < 2 * STEPS - 1)
         def _():
             pack_halo(step + 1)
             for side in range(2):
                 halo_copy(step + 1, side).start()
+
+        @pl.when(step == STEPS - 1)
+        def _():
+            follow_copy(1, first_ref).start()
 
         return carry
 
@@ -317,20 +401,30 @@
     first_image, second_image = pl.pallas_call(
         functools.partial(kernel, lax.axis_size("seg"), lax.axis_size("elem")),
         out_shape=(field, field),
-        in_specs=[vmem] * 8,
+        in_specs=[pl.BlockSpec(memory_space=pltpu.HBM)] * 8,
         out_specs=(vmem, vmem),
         scratch_shapes=[
+            pltpu.VMEM((COMP, NODES, SHARD), jnp.float32),
+            pltpu.VMEM((COMP, NODES, SHARD), jnp.float32),
+            pltpu.VMEM((6, SHARD), jnp.int32),
+            pltpu.VMEM((6, SHARD), jnp.int32),
+            pltpu.VMEM((1, SHARD), jnp.int32),
+            pltpu.VMEM(operators.shape, jnp.bfloat16),
+            pltpu.VMEM(select.shape, jnp.bfloat16),
+            pltpu.VMEM(lift.shape, jnp.bfloat16),
             pltpu.VMEM((COMP * NODES, SHARD), jnp.float32),
             pltpu.VMEM((COMP, NODES, SHARD), jnp.float32),
             pltpu.VMEM((3, COMP, NODES, SHARD), jnp.float32),
             pltpu.VMEM((NODES, SHARD), jnp.float32),
-            pltpu.VMEM((2, 2, CODES, LANES, LANES), jnp.bfloat16),
-            pltpu.VMEM((CODES, 2 * COMP, 16, SHARD), jnp.bfloat16),
+            pltpu.VMEM((CODES, SHARD, SHARD), jnp.bfloat16),
+            pltpu.VMEM((CODES, LANES, SHARD), jnp.bfloat16),
+            pltpu.VMEM((TRACES, 16 * COMP, SHARD), jnp.bfloat16),
+            pltpu.VMEM((TRACES, 16 * COMP, LANES), jnp.bfloat16),
             pltpu.VMEM((COMP, 96, SHARD), jnp.float32),
-            pltpu.VMEM((COMP * NODES, SHARD), jnp.float32),
             pltpu.VMEM((2 * STEPS, 2, 96, LANES), jnp.float32),
             pltpu.VMEM((2 * STEPS, 2, 96, LANES), jnp.float32),
             pltpu.VMEM((2, COMP, NODES, SHARD), jnp.float32),
+            pltpu.SemaphoreType.DMA((8,)),
             pltpu.SemaphoreType.DMA((2 * STEPS, 2)),
             pltpu.SemaphoreType.DMA((2 * STEPS, 2)),
             pltpu.SemaphoreType.DMA((2,)),
@@ -341,14 +435,19 @@
         ),
         name="shooting",
     )(
-        base_flow[0],
-        probe_field[0],
-        neighbours,
-        face_codes,
-        face_counts.reshape(1, SHARD),
-        operators,
-        select,
-        lift,
+        *[
+            pltpu.with_memory_space_constraint(value, pltpu.HBM)
+            for value in (
+                base_flow[0],
+                probe_field[0],
+                neighbours,
+                face_codes,
+                face_counts.reshape(1, SHARD),
+                operators,
+                select,
+                lift,
+            )
+        ]
     )
     return (first_image[None], second_image[None])
 

time: 37.1 us -> 28.9 us (0.78)
  local copies, waits for them, and re-layouts: 7.83 us -> 1.36 us
  Pallas kernels: 28.2 us -> 26.8 us
    unnamed x18 -> x2, local copies, waits for them, and re-layouts: 7.83 us -> 1.36 us
    pallas_call x1, Pallas kernels: 28.2 us -> 26.8 us  [on_device(): pl.pallas_call(functools.partial(kernel, lax.axis_size('seg'), lax.axis_s...]
where the time goes in v1:
time: 28.9 us; the launch traced here: 28.8 us
  Pallas kernels  26.8 us (93%)
  local copies, waits for them, and re-layouts  1.36 us (5%)
  between operations  0.64 us (2%)
    pallas_call x1, Pallas kernels, on_device(): pl.pallas_call(functools.partial(kernel, lax.axis_size('seg'), lax.axis_s...  26.8 us
    unnamed x2, local copies, waits for them, and re-layouts  1.36 us

profile of v1, /device:TPU:2, one launch (start us, length us, event | category | flops | bytes accessed | tf_op | source)
XLA Modules:
  0.0 28.8 jit_solution(9490859734639200342)
XLA Ops:
  0.6 26.8 %shooting.1 = (f32[3,64,256]{2,1,0:T(8,128)S(1)}, f32[3,64,256]{2,1,0:T(8,128)S(1)}) custom-call(f32[3,64,256]{2,1,0:T(8,128)} %bitcast.7, f32[3,64,256]{2,1,0:T(8,128)} %bitcast.8, s32[6,256]{1,0:T(8,128)} %near_in.1, s32[6,256]{1,0:T(8,128)} %code_in.1, s32[1,256]{1,0:T(1,128)} %bitcast.9, bf16[256,256]{1,0:T(8,128)(2,1)} %constant.6.clone.oper_in, ...), custom_call_target="tpu_custom_call" | custom-call | tf_op jit(solution)/shard_map/shooting/pallas_call | solution.py:401
  27.4 0.7 %copy.12 = f32[1,3,64,256]{3,2,1,0:T(8,128)} copy(f32[1,3,64,256]{3,2,1,0:T(8,128)S(1)} %bitcast.6) | data formatting | bytes 393216
  28.1 0.7 %copy.13 = f32[1,3,64,256]{3,2,1,0:T(8,128)} copy(f32[1,3,64,256]{3,2,1,0:T(8,128)S(1)} %bitcast.5) | data formatting | bytes 393216

commit v2 on v1

v2 whole, which is shorter than its diff:
```python
import functools

import jax
import jax.numpy as jnp
import ml_dtypes
import numpy as np
from jax import lax
from jax.experimental import pallas as pl
from jax.experimental.pallas import tpu as pltpu
from jax.sharding import PartitionSpec as P

STEPS = 2
VISCOSITY = 0.05
PENALTY = 1.0
TIME_STEP = 0.05

COMP = 3
NODES = 64
SHARD = 256
LANES = 128
HALO = 64
TRACES = 24


def operator_tables():
    points = np.array([-1.0, -1.0 / np.sqrt(5.0), 1.0 / np.sqrt(5.0), 1.0])
    barycentric = np.array(
        [
            1.0 / np.prod([points[row] - points[col] for col in range(4) if col != row])
            for row in range(4)
        ]
    )
    derivative = np.zeros((4, 4))
    for row in range(4):
        for col in range(4):
            if row != col:
                derivative[row, col] = (
                    barycentric[col] / barycentric[row] / (points[row] - points[col])
                )
        derivative[row, row] = -np.sum(derivative[row])
    identity = np.eye(4)
    gradient = [
        np.kron(np.kron(derivative, identity), identity),
        np.kron(np.kron(identity, derivative), identity),
        np.kron(np.kron(identity, identity), derivative),
    ]
    laplacian = sum(table @ table for table in gradient)
    return gradient, laplacian


def face_nodes(which_face):
    grid = np.arange(NODES).reshape(4, 4, 4)
    return np.take(grid, 0 if which_face % 2 == 0 else 3, axis=which_face // 2)


def orbit_places():
    turned = np.rot90(np.arange(16).reshape(4, 4), 1).ravel()
    seen, starts = set(), []
    for place in range(16):
        if place not in seen:
            starts.append(place)
            for _ in range(4):
                seen.add(place)
                place = turned[place]
    rows = [starts]
    for _ in range(3):
        rows.append([turned[place] for place in rows[-1]])
    return np.array(rows).ravel()


def constant_tables():
    gradient, laplacian = operator_tables()
    stacked = np.concatenate([VISCOSITY * laplacian] + gradient, axis=0)
    high = stacked.astype(ml_dtypes.bfloat16)
    low = (stacked - high.astype(np.float64)).astype(ml_dtypes.bfloat16)
    operators = np.concatenate([high, high, low, low], axis=1)
    places = orbit_places()
    select = np.zeros((2, 6, 2, 2, 8, 2, NODES))
    lift = np.zeros((NODES, 96))
    for face in range(6):
        source = face_nodes(face ^ 1).ravel()[places]
        target = face_nodes(face).ravel()[places]
        for turn in range(2):
            for place in range(16):
                node = source[(place + 4 * turn) % 16]
                for piece in range(2):
                    select[turn, face, place // 8, piece, place % 8, piece, node] = 1.0
        for place in range(16):
            lift[target[place], face * 16 + place] = 1.0
    select = select.reshape(TRACES * 16, 2 * NODES)
    paired = np.concatenate([select[: TRACES * 8], select[TRACES * 8 :]], axis=1)
    lift = np.concatenate([lift, lift], axis=1)
    return (
        jnp.asarray(operators),
        jnp.asarray(select.astype(ml_dtypes.bfloat16)),
        jnp.asarray(paired.astype(ml_dtypes.bfloat16)),
        jnp.asarray(lift.astype(ml_dtypes.bfloat16)),
    )


def split(value):
    high = value.astype(jnp.bfloat16)
    low = (value - high.astype(jnp.float32)).astype(jnp.bfloat16)
    return high, low


def dot(left, right):
    return jnp.dot(left, right, preferred_element_type=jnp.float32)


def kernel(
    segs,
    elems,
    base_in,
    probe_in,
    near_in,
    code_in,
    count_in,
    oper_in,
    sel_in,
    pair_in,
    lift_in,
    first_ref,
    second_ref,
    base_ref,
    probe_ref,
    near_ref,
    code_ref,
    count_ref,
    oper_ref,
    sel_ref,
    pair_ref,
    lift_ref,
    state,
    acc,
    base_grad,
    own_count,
    hot,
    inner,
    outer,
    trace_own,
    trace_cross,
    jumps,
    send_buf,
    halo_buf,
    follow,
    input_sem,
    halo_send,
    halo_recv,
    follow_send,
    follow_recv,
):
    seg = lax.axis_index("seg")
    elem = lax.axis_index("elem")
    right = lax.rem(elem + 1, elems)
    left = lax.rem(elem + elems - 1, elems)
    ahead = lax.rem(seg + 1, segs)
    behind = lax.rem(seg + segs - 1, segs)
    barrier = pltpu.get_barrier_semaphore()
    for target in ({"elem": left}, {"elem": right}, {"seg": ahead}):
        pl.semaphore_signal(
            barrier, inc=1, device_id=target, device_id_type=pl.DeviceIdType.MESH
        )
    loads = [
        pltpu.make_async_copy(source, target, input_sem.at[index])
        for index, (source, target) in enumerate(
            (
                (near_in, near_ref),
                (code_in, code_ref),
                (count_in, count_ref),
                (probe_in, probe_ref),
                (base_in, base_ref),
                (oper_in, oper_ref),
                (sel_in, sel_ref),
                (pair_in, pair_ref),
                (lift_in, lift_ref),
            )
        )
    ]
    for load in loads:
        load.start()

    block_lanes = (slice(0, LANES), slice(LANES, SHARD))
    lane_low = lax.broadcasted_iota(jnp.int32, (96, LANES), 1) < HALO
    low_ones = lax.broadcasted_iota(jnp.int32, (16, LANES), 1) < HALO
    low_ones = jnp.where(low_ones, 1.0, 0.0).astype(jnp.bfloat16)
    keep_high = jnp.concatenate([1.0 - low_ones] * 8, axis=0)
    keep_low = jnp.concatenate([low_ones] * 8, axis=0)

    def halo_copy(step, block):
        return pltpu.make_async_remote_copy(
            src_ref=send_buf.at[step, block],
            dst_ref=halo_buf.at[step, 1 - block],
            send_sem=halo_send.at[step, block],
            recv_sem=halo_recv.at[step, 1 - block],
            device_id={"elem": (left, right)[block]},
            device_id_type=pl.DeviceIdType.MESH,
        )

    def pack_halo(step, block):
        lanes = block_lanes[block]
        upper, lower = state[0:96, lanes], pltpu.roll(state[96:192, lanes], HALO, 1)
        send_buf[step, block] = (
            jnp.where(lane_low, upper, lower)
            if block == 0
            else jnp.where(lane_low, lower, upper)
        )

    def follow_copy(image, source):
        return pltpu.make_async_remote_copy(
            src_ref=source,
            dst_ref=follow.at[image],
            send_sem=follow_send.at[image],
            recv_sem=follow_recv.at[image],
            device_id={"seg": behind},
            device_id_type=pl.DeviceIdType.MESH,
        )

    for load in loads[0:3]:
        load.wait()
    first_block = elem * (SHARD // LANES)
    row = lax.broadcasted_iota(jnp.int32, (LANES, LANES), 0)
    codes = []
    for block in range(2):
        lanes = block_lanes[block]
        slot = lax.broadcasted_iota(jnp.int32, (6, LANES), 0)
        codes.append(jnp.where(slot < count_ref[:, lanes], code_ref[:, lanes], -1))
        place = jnp.bitwise_and(near_ref[:, lanes], LANES - 1)
        is_own = jnp.right_shift(near_ref[:, lanes], 7) == first_block + block
        for part, chosen in enumerate(
            (jnp.where(is_own, place, -1), jnp.where(is_own, -1, place))
        ):
            for k in range(6):
                hot[block, part, k] = jnp.where(row == chosen[k : k + 1], 1.0, 0.0).astype(
                    jnp.bfloat16
                )

    loads[3].wait()
    state[...] = probe_ref[...].reshape(COMP * NODES, SHARD)
    for block in range(2):
        pack_halo(0, block)
    pl.semaphore_wait(barrier, 3)
    for block in range(2):
        halo_copy(0, block).start()
    follow_copy(0, probe_ref).start()

    wide_codes = [
        [jnp.broadcast_to(codes[block][k : k + 1], (8, LANES)) for k in range(6)]
        for block in range(2)
    ]

    def build(face, carry):
        for block in range(2):
            matches = []
            for turn in range(4):
                matches.append([])
                for k in range(6):
                    match = jnp.where(wide_codes[block][k] == 4 * face + turn, 1.0, 0.0)
                    match = jnp.concatenate([match, match], axis=0).astype(jnp.bfloat16)
                    matches[turn].append(match)
            for part in range(2):
                for chunk in range(8):
                    rows = [hot[block, part, k, 16 * chunk : 16 * chunk + 16] for k in range(6)]
                    for turn in range(4):
                        total = rows[0] * matches[turn][0]
                        for k in range(1, 6):
                            total = total + rows[k] * matches[turn][k]
                        if part == 0:
                            at = LANES * turn + 16 * chunk
                            inner[block, face, at : at + 16] = total
                        elif (chunk < 4) == (block == 0):
                            at = 4 * LANES + HALO * turn + 16 * (chunk % 4)
                            inner[block, face, at : at + 16] = total
                        else:
                            at = HALO * turn + 16 * (chunk % 4)
                            outer[block, face, at : at + 16] = total
        return carry

    lax.fori_loop(0, 6, build, 0)

    node = lax.broadcasted_iota(jnp.int32, (NODES, LANES), 0)
    digits = (
        jnp.right_shift(node, 4),
        jnp.bitwise_and(jnp.right_shift(node, 2), 3),
        jnp.bitwise_and(node, 3),
    )
    for block in range(2):
        code = codes[block]
        total = jnp.zeros((NODES, LANES), jnp.float32)
        for face in range(6):
            hits = jnp.zeros((1, LANES), jnp.float32)
            for k in range(6):
                match = jnp.logical_and(
                    code[k : k + 1] >= 4 * face, code[k : k + 1] < 4 * face + 4
                )
                hits = hits + jnp.where(match, 1.0, 0.0)
            on_face = digits[face // 2] == (0 if face % 2 == 0 else 3)
            total = total + jnp.where(on_face, hits, 0.0)
        own_count[:, block_lanes[block]] = total

    for load in loads[4:]:
        load.wait()

    def stacked(value):
        return jnp.concatenate(split(value), axis=0)

    def derivatives(pieces):
        return dot(oper_ref[...], jnp.concatenate([pieces, pieces], axis=0))

    for comp in range(COMP):
        grads = derivatives(stacked(base_ref[comp]))
        for d in range(3):
            base_grad[d, comp] = grads[(d + 1) * NODES : (d + 2) * NODES]

    def fill_pairs(comp, at_low, at_high):
        paired = jnp.concatenate([at_low * keep_low, at_high * keep_high], axis=0)
        picked = dot(pair_ref[...], paired).astype(jnp.bfloat16)
        return picked.reshape(TRACES // 2, 16, LANES)

    def stacked_halves(halves, face, turns):
        pair = 2 * face + 12 * (turns % 2)
        first = pair + turns // 2
        return jnp.concatenate([halves(first), halves(2 * pair + 1 - first)], axis=0)

    def add_pieces(found, comp, half):
        at = 48 * half + 16 * comp
        return found[at : at + 8] + found[at + 8 : at + 16]

    def before_halo():
        for comp in range(COMP):
            field = state[comp * NODES : (comp + 1) * NODES]
            pieces = stacked(field)
            grads = derivatives(pieces)
            total = grads[0:NODES] - own_count[...] * field
            for d in range(3):
                total = total - base_ref[d] * grads[(d + 1) * NODES : (d + 2) * NODES]
            for d in range(3):
                total = total - state[d * NODES : (d + 1) * NODES] * base_grad[d, comp]
            acc[comp] = total
            rows = slice(16 * comp, 16 * comp + 16)
            picked = dot(sel_ref[...], pieces).astype(jnp.bfloat16)
            trace_own[:, rows] = picked.reshape(TRACES, 16, SHARD)
            turned = [stacked(pltpu.roll(field[:, lanes], HALO, 1)) for lanes in block_lanes]
            trace_cross[0, :, rows] = fill_pairs(comp, pieces[:, LANES:SHARD], turned[1])
            trace_cross[1, :, rows] = fill_pairs(comp, turned[0], pieces[:, 0:LANES])
        for block in range(2):
            lanes = block_lanes[block]
            for face in range(6):
                sources = [
                    stacked_halves(lambda at: trace_own[at, :, lanes], face, turn)
                    for turn in range(4)
                ]
                for turn in (0, 2):
                    sources.append(
                        stacked_halves(lambda at: trace_cross[block, at], face, turn)
                    )
                found = dot(jnp.concatenate(sources, axis=1), inner[block, face])
                for half in range(2):
                    at = 16 * face + 8 * half
                    for comp in range(COMP):
                        jumps[comp, at : at + 8, lanes] = add_pieces(found, comp, half)

    def after_halo(step, block):
        lanes = block_lanes[block]
        halo_copy(step, 1 - block).wait_recv()
        packet = halo_buf[step, block]
        turned = pltpu.roll(packet, HALO, 1)
        as_sent = jnp.concatenate([packet, turned], axis=0)
        shifted = jnp.concatenate([turned, packet], axis=0)
        at_high, at_low = (as_sent, shifted) if block == 0 else (shifted, as_sent)
        traces = []
        for comp in range(COMP):
            rows = slice(comp * NODES, (comp + 1) * NODES)
            traces.append(fill_pairs(comp, stacked(at_low[rows]), stacked(at_high[rows])))
        totals = [[] for comp in range(COMP)]
        for face in range(6):
            sources = [
                stacked_halves(
                    lambda at: jnp.concatenate([trace[at] for trace in traces], axis=0),
                    face,
                    turn,
                )
                for turn in (0, 2)
            ]
            found = dot(jnp.concatenate(sources, axis=1), outer[block, face])
            for half in range(2):
                at = 16 * face + 8 * half
                for comp in range(COMP):
                    totals[comp].append(
                        add_pieces(found, comp, half) + jumps[comp, at : at + 8, lanes]
                    )
        last = step % STEPS == STEPS - 1
        image = step // STEPS
        result = (first_ref, second_ref)[image]
        for comp in range(COMP):
            flux = dot(lift_ref[...], stacked(jnp.concatenate(totals[comp], axis=0)))
            rows = slice(comp * NODES, (comp + 1) * NODES)
            value = state[rows, lanes]
            value = value + TIME_STEP * (acc[comp, :, lanes] + PENALTY * flux)
            if last:
                value = value - follow[image, comp, :, lanes]
                result[comp, :, lanes] = value
            if step < 2 * STEPS - 1:
                state[rows, lanes] = value
        if step < 2 * STEPS - 1:
            pack_halo(step + 1, block)
            halo_copy(step + 1, block).start()

    for step in range(2 * STEPS):
        before_halo()
        if step % STEPS == STEPS - 1:
            follow_copy(step // STEPS, first_ref).wait_recv()
        for block in (step % 2, 1 - step % 2):
            after_halo(step, block)
        if step == STEPS - 1:
            follow_copy(1, first_ref).start()
    for step in range(2 * STEPS):
        for block in range(2):
            halo_copy(step, block).wait_send()
    for image, source in enumerate((probe_ref, first_ref)):
        follow_copy(image, source).wait_send()


def on_device(base_flow, probe_field, neighbours, face_codes, face_counts):
    operators, select, paired, lift = constant_tables()
    field = jax.ShapeDtypeStruct((COMP, NODES, SHARD), jnp.float32)
    vmem = pl.BlockSpec(memory_space=pltpu.VMEM)
    first_image, second_image = pl.pallas_call(
        functools.partial(kernel, lax.axis_size("seg"), lax.axis_size("elem")),
        out_shape=(field, field),
        in_specs=[pl.BlockSpec(memory_space=pltpu.HBM)] * 9,
        out_specs=(vmem, vmem),
        scratch_shapes=[
            pltpu.VMEM((COMP, NODES, SHARD), jnp.float32),
            pltpu.VMEM((COMP, NODES, SHARD), jnp.float32),
            pltpu.VMEM((6, SHARD), jnp.int32),
            pltpu.VMEM((6, SHARD), jnp.int32),
            pltpu.VMEM((1, SHARD), jnp.int32),
            pltpu.VMEM(operators.shape, jnp.bfloat16),
            pltpu.VMEM(select.shape, jnp.bfloat16),
            pltpu.VMEM(paired.shape, jnp.bfloat16),
            pltpu.VMEM(lift.shape, jnp.bfloat16),
            pltpu.VMEM((COMP * NODES, SHARD), jnp.float32),
            pltpu.VMEM((COMP, NODES, SHARD), jnp.float32),
            pltpu.VMEM((3, COMP, NODES, SHARD), jnp.float32),
            pltpu.VMEM((NODES, SHARD), jnp.float32),
            pltpu.VMEM((2, 2, 6, LANES, LANES), jnp.bfloat16),
            pltpu.VMEM((2, 6, 4 * (LANES + HALO), LANES), jnp.bfloat16),
            pltpu.VMEM((2, 6, 4 * HALO, LANES), jnp.bfloat16),
            pltpu.VMEM((TRACES, 16 * COMP, SHARD), jnp.bfloat16),
            pltpu.VMEM((2, TRACES // 2, 16 * COMP, LANES), jnp.bfloat16),
            pltpu.VMEM((COMP, 96, SHARD), jnp.float32),
            pltpu.VMEM((2 * STEPS, 2, 96, LANES), jnp.float32),
            pltpu.VMEM((2 * STEPS, 2, 96, LANES), jnp.float32),
            pltpu.VMEM((2, COMP, NODES, SHARD), jnp.float32),
            pltpu.SemaphoreType.DMA((9,)),
            pltpu.SemaphoreType.DMA((2 * STEPS, 2)),
            pltpu.SemaphoreType.DMA((2 * STEPS, 2)),
            pltpu.SemaphoreType.DMA((2,)),
            pltpu.SemaphoreType.DMA((2,)),
        ],
        compiler_params=pltpu.CompilerParams(
            collective_id=0, has_side_effects=True, vmem_limit_bytes=40 * 1024 * 1024
        ),
        name="shooting",
    )(
        *[
            pltpu.with_memory_space_constraint(value, pltpu.HBM)
            for value in (
                base_flow[0],
                probe_field[0],
                neighbours,
                face_codes,
                face_counts.reshape(1, SHARD),
                operators,
                select,
                paired,
                lift,
            )
        ]
    )
    return (first_image[None], second_image[None])


def solution(mesh):
    placed = (
        P("seg", None, None, "elem"),
        P("seg", None, None, "elem"),
        P(None, "elem"),
        P(None, "elem"),
        P("elem"),
    )
    return jax.shard_map(
        on_device,
        mesh=mesh,
        in_specs=placed,
        out_specs=(P("seg", None, None, "elem"), P("seg", None, None, "elem")),
        check_vma=False,
    )
```

time: 28.9 us -> 29.8 us (1.031)
  Pallas kernels: 26.8 us -> 27.7 us
    pallas_call x1, Pallas kernels: 26.8 us -> 27.7 us  [on_device(): pl.pallas_call(functools.partial(kernel, lax.axis_size('seg'), lax.axis_s...]
where the time goes in v2:
time: 29.8 us; the launch traced here: 29.7 us
  Pallas kernels  27.7 us (93%)
  local copies, waits for them, and re-layouts  1.36 us (5%)
  between operations  0.64 us (2%)
    pallas_call x1, Pallas kernels, on_device(): pl.pallas_call(functools.partial(kernel, lax.axis_size('seg'), lax.axis_s...  27.7 us
    unnamed x2, local copies, waits for them, and re-layouts  1.36 us

profile of v2, /device:TPU:2, one launch (start us, length us, event | category | flops | bytes accessed | tf_op | source)
XLA Modules:
  0.0 29.7 jit_solution(3614305883596744523)
XLA Ops:
  0.6 27.7 %shooting.1 = (f32[3,64,256]{2,1,0:T(8,128)S(1)}, f32[3,64,256]{2,1,0:T(8,128)S(1)}) custom-call(f32[3,64,256]{2,1,0:T(8,128)} %bitcast.7, f32[3,64,256]{2,1,0:T(8,128)} %bitcast.8, s32[6,256]{1,0:T(8,128)} %near_in.1, s32[6,256]{1,0:T(8,128)} %code_in.1, s32[1,256]{1,0:T(1,128)} %bitcast.9, bf16[256,256]{1,0:T(8,128)(2,1)} %constant.8.clone.oper_in, ...), custom_call_target="tpu_custom_call" | custom-call | tf_op jit(solution)/shard_map/shooting/pallas_call | solution.py:428
  28.3 0.7 %copy.13 = f32[1,3,64,256]{3,2,1,0:T(8,128)} copy(f32[1,3,64,256]{3,2,1,0:T(8,128)S(1)} %bitcast.6) | data formatting | bytes 393216
  29.0 0.7 %copy.14 = f32[1,3,64,256]{3,2,1,0:T(8,128)} copy(f32[1,3,64,256]{3,2,1,0:T(8,128)S(1)} %bitcast.5) | data formatting | bytes 393216
